TPU v7x, 32 devices: a whole 2x2x4 slice. The times are simulated.
32 devices in a mesh: dp: 4 (over y, x), ep: 8 (over z, core).
Axes of the slice: x: 2, y: 2, z: 4, core: 2. Of those that a mesh axis runs over, the one named last changes fastest.
Arguments:
- attn_heads: bfloat16 [8, 256, 2048], P('ep', None, 'dp'), may hold values from -6 to 6
- residual: bfloat16 [8, 256, 2048], P('ep', 'dp'), may hold values from -6 to 6
- w_out: bfloat16 [2048, 2048], P('dp'), may hold values from -0.125 to 0.125
- gain_post: bfloat16 [2048], replicated, may hold values from 0.5 to 1.5
- w_router: bfloat16 [2048, 60], replicated, may hold values from -0.125 to 0.125
- expert_ids: int32 [8, 256, 4], P('ep', 'dp'), may hold values from 0 to 59, all different within a row; in each aligned block of 64 rows (0 to 63, 64 to 127, ..., all dimensions but the last counted through in order) at most 8 rows name the same one
- expert_slot: int32 [60], replicated, may hold values from 0 to 63, as said below
- w_gate: bfloat16 [64, 2048, 1408], P('ep', None, 'dp'), may hold values from -0.125 to 0.125
- w_up: bfloat16 [64, 2048, 1408], P('ep', None, 'dp'), may hold values from -0.125 to 0.125
- w_down: bfloat16 [64, 1408, 2048], P('ep', 'dp'), may hold values from -0.15625 to 0.15625
- w_shared_gate: bfloat16 [2048, 5632], P(None, 'ep'), may hold values from -0.125 to 0.125
- w_shared_up: bfloat16 [2048, 5632], P(None, 'ep'), may hold values from -0.125 to 0.125
- w_shared_down: bfloat16 [5632, 2048], P('ep'), may hold values from -0.078125 to 0.078125
- w_shared_score: bfloat16 [2048], replicated, may hold values from -0.125 to 0.125
- gain_final: bfloat16 [2048], replicated, may hold values from 0.5 to 1.5
Outputs:
- mixed_out: bfloat16 [8, 256, 2048], P('ep', 'dp')
- final_out: bfloat16 [8, 256, 2048], P('ep', 'dp')
Inputs may be any that keep to these rules, and one draw needn't show every extreme that they name: `expert_ids`: each row names 4 different experts. Within the 64 rows of one device no expert is named by more than 8 rows, and in some device one expert is named by exactly 8 rows. All entries differ; expert e uses entry expert_slot[e] of w_gate, w_up and w_down, and index i of ep holds positions i * 8 to (i + 1) * 8 - 1.
All inputs are finite; a program needn't handle non-finite values.
Results may differ from a plain program's by a relative error of at most 0.02.
Values may be sent and summed in bfloat16 or wider, within the bound.
A program may use at most 128 MiB of HBM per device.

v0:
```python
import jax
import jax.numpy as jnp
from jax import lax
from jax.sharding import PartitionSpec as P

MOST = 8
eps_norm = 1e-06


def rms_scale(values_in, gain_vec):
    values = values_in.astype(jnp.float32)
    return (
        values
        * lax.rsqrt(jnp.mean(values * values, axis=-1, keepdims=True) + eps_norm)
        * gain_vec.astype(jnp.float32)
    )


def expert_partial(rows_in, w_gate, w_up, w_down):
    gate_part = jnp.einsum("semd,edf->semf", rows_in, w_gate, preferred_element_type=jnp.float32)
    up_part = jnp.einsum("semd,edf->semf", rows_in, w_up, preferred_element_type=jnp.float32)
    hidden = (jax.nn.silu(gate_part) * up_part).astype(jnp.bfloat16)
    return jnp.einsum("semf,efd->semd", hidden, w_down, preferred_element_type=jnp.float32)


def per_device(
    attn_heads,
    residual,
    w_out,
    gain_post,
    w_router,
    expert_ids,
    expert_slot,
    w_gate,
    w_up,
    w_down,
    w_shared_gate,
    w_shared_up,
    w_shared_down,
    w_shared_score,
    gain_final,
):
    local_heads = attn_heads[0]
    model_width = residual.shape[2]
    row_block = local_heads
    projected = lax.psum_scatter(
        jnp.dot(row_block, w_out, preferred_element_type=jnp.float32).astype(jnp.bfloat16),
        "dp",
        scatter_dimension=0,
        tiled=True,
    ).astype(jnp.float32)
    hidden_state = (residual[0].astype(jnp.float32) + projected).astype(jnp.bfloat16)
    normed = rms_scale(hidden_state, gain_post).astype(jnp.bfloat16)
    logits = jnp.dot(normed, w_router, preferred_element_type=jnp.float32)
    chosen = expert_ids[0]
    expert_count = w_router.shape[1]
    one_hot = chosen[:, :, None] == jnp.arange(expert_count, dtype=jnp.int32)[None, None, :]
    picked = jnp.sum(jnp.where(one_hot, logits[:, None, :], 0.0), axis=2)
    exp_logits = jnp.exp(picked)
    route_weights = (exp_logits / jnp.sum(exp_logits, axis=1, keepdims=True)).astype(jnp.bfloat16)
    experts_here = w_gate.shape[0]
    groups = lax.axis_size("ep")
    positions = experts_here * groups
    buffer_cells = positions * MOST
    expert_hits = jnp.any(one_hot, axis=1).astype(jnp.int32)
    earlier = jnp.cumsum(expert_hits, axis=0) - expert_hits
    slot_rank = jnp.sum(jnp.where(one_hot, earlier[:, None, :], 0), axis=2)
    position = jnp.sum(jnp.where(one_hot, expert_slot[None, None, :], 0), axis=2)
    buffer_index = position * MOST + slot_rank
    placed = buffer_index[:, :, None] == jnp.arange(buffer_cells, dtype=jnp.int32)[None, None, :]
    dispatch_mat = jnp.any(placed, axis=1).astype(jnp.bfloat16)
    combine_mat = jnp.sum(
        jnp.where(placed, route_weights.astype(jnp.float32)[:, :, None], 0.0), axis=1
    ).astype(jnp.bfloat16)
    outgoing = jnp.einsum(
        "rc,rd->cd", dispatch_mat, normed, preferred_element_type=jnp.float32
    ).astype(jnp.bfloat16)
    outgoing = outgoing.reshape(groups, experts_here, MOST, model_width)
    dp_count = lax.axis_size("dp")
    copies = jnp.broadcast_to(outgoing[None], (dp_count,) + outgoing.shape).reshape(
        (dp_count * groups, experts_here, MOST, model_width)
    )
    partial_value = expert_partial(
        lax.all_to_all(copies, ("dp", "ep"), split_axis=0, concat_axis=0, tiled=True),
        w_gate,
        w_up,
        w_down,
    ).astype(jnp.bfloat16)
    returned_all = lax.all_to_all(
        partial_value, ("dp", "ep"), split_axis=0, concat_axis=0, tiled=True
    )
    returned = jnp.sum(
        returned_all.reshape(dp_count, groups, experts_here, MOST, model_width).astype(jnp.float32),
        axis=0,
    ).astype(jnp.bfloat16)
    routed = jnp.dot(
        combine_mat, returned.reshape(buffer_cells, model_width), preferred_element_type=jnp.float32
    )
    row_block = lax.all_gather(normed, "ep", axis=0, tiled=True)
    gate_part = jnp.dot(row_block, w_shared_gate, preferred_element_type=jnp.float32)
    up_part = jnp.dot(row_block, w_shared_up, preferred_element_type=jnp.float32)
    hidden_all = (jax.nn.silu(gate_part) * up_part).astype(jnp.bfloat16)
    row_block = hidden_all
    shared_sum = lax.psum_scatter(
        jnp.dot(row_block, w_shared_down, preferred_element_type=jnp.float32).astype(jnp.bfloat16),
        "ep",
        scatter_dimension=0,
        tiled=True,
    ).astype(jnp.float32)
    shared_score = jax.nn.sigmoid(
        jnp.dot(normed, w_shared_score, preferred_element_type=jnp.float32)
    )
    mixed_out = (
        hidden_state.astype(jnp.float32) + shared_score[:, None] * shared_sum + routed
    ).astype(jnp.bfloat16)
    final_out = rms_scale(mixed_out, gain_final).astype(jnp.bfloat16)
    return (mixed_out[None], final_out[None])


def solution(mesh):
    in_specs = (
        P("ep", None, "dp"),
        P("ep", "dp", None),
        P("dp", None),
        P(),
        P(),
        P("ep", "dp", None),
        P(),
        P("ep", None, "dp"),
        P("ep", None, "dp"),
        P("ep", "dp", None),
        P(None, "ep"),
        P(None, "ep"),
        P("ep", None),
        P(),
        P(),
    )
    out_specs = (P("ep", "dp", None), P("ep", "dp", None))
    return jax.shard_map(
        per_device, mesh=mesh, in_specs=in_specs, out_specs=out_specs, check_vma=False
    )
```

profile of v0, /device:TPU:0, one launch (start us, length us, event | category | flops | bytes accessed | tf_op | source)
XLA Modules:
  0.0 522.7 jit_solution(2066058382093305351)
XLA Ops:
  7.2 0.0 copy-start
  7.2 0.0 copy-start.6
  7.2 0.0 copy-start.7
  7.2 0.0 copy-start.10
  7.2 0.0 copy-start.3
  7.2 0.0 reduce-scatter.3.cloned.1.call-start
  7.3 3.5 convolution_convert_fusion.2
  10.8 0.0 reduce-scatter.3.cloned.1.call-update
  10.8 0.0 copy-done.6
  10.8 0.1 fusion.38
  10.9 0.1 copy.29
  11.1 0.1 reduce_window_sum.11
  11.2 0.1 copy.30
  11.2 0.0 copy-done.7
  11.3 0.0 copy-done.10
  11.3 0.1 select_reduce_fusion.3
  11.4 0.1 fusion.31
  11.6 29.8 %reduce-scatter.3.cloned.1.call-done = bf16[64,2048]{1,0:T(8,128)(2,1)} async-done(((bf16[256,2048]{1,0:T(8,128)(2,1)}), bf16[64,2048]{1,0:T(8,128)(2,1)}) %reduce-scatter.3.cloned.1.call-update) | async-done | bytes 262160 | tf_op jit(solution)/shard_map/reduce_scatter | solution.py:46
  41.4 0.0 copy-done.3
  41.4 1.1 fusion.27
  42.5 1.1 fusion.29
  43.6 0.0 copy-start.1
  43.6 0.8 convolution_convert_fusion
  44.4 1.1 broadcast_in_dim.80
  45.5 0.0 copy-done.1
  45.5 189.4 %all_to_all.10 = bf16[32,8,8,2048]{3,2,1,0:T(8,128)(2,1)} all-to-all(bf16[32,8,8,2048]{3,2,1,0:T(8,128)(2,1)S(1)} %bitcast.88), channel_id=1, replica_groups=mesh['dp'=4,'ep'=8] {'dp','ep'}, dimensions={0} | all-to-all | bytes 16777216 | tf_op jit(solution)/shard_map/all_to_all | solution.py:84
  234.9 14.1 %fusion.4 = f32[8,32,8,352]{3,2,1,0:T(8,128)} fusion(bf16[8,2048,352]{1,2,0:T(8,128)(2,1)} %param.22, bf16[32,8,8,2048]{3,2,1,0:T(8,128)(2,1)} %all_to_all.10), kind=kOutput, calls=%fused_computation.4 | convolution fusion | flops 2952790016 | bytes 22806528 | tf_op jit(solution)/shard_map/semd,edf->semf/dot_general | solution.py:20
  249.0 23.5 %convert_bitcast_fusion = bf16[32,8,8,2048]{3,2,0,1:T(8,128)(2,1)} fusion(bf16[8,352,2048]{2,1,0:T(8,128)(2,1)} %param.24, f32[8,32,8,352]{3,2,1,0:T(8,128)} %fusion.4, bf16[8,2048,352]{1,2,0:T(8,128)(2,1)} %param.23, bf16[32,8,8,2048]{3,2,1,0:T(8,128)(2,1)} %all_to_all.10), kind=kOutput, calls=%fused_computation.6 | convolution fusion | flops 5914099712 | bytes 42729472 | tf_op jit(solution)/shard_map/semf,efd->semd/dot_general | solution.py:23
  272.5 8.3 %copy.34 = bf16[32,8,8,2048]{3,2,1,0:T(8,128)(2,1)} copy(bf16[32,8,8,2048]{3,2,0,1:T(8,128)(2,1)} %convert_bitcast_fusion) | data formatting | bytes 16777216 | tf_op jit(solution)/shard_map/convert_element_type | solution.py:88
  280.7 3.7 all-to-all-start.1
  284.4 0.0 all-gather.2.cloned.1.call-start
  284.5 0.7 all-gather.2.cloned.1.call-update
  285.2 0.2 reduce-scatter.5.cloned.1.call-start
  285.4 52.7 %all-gather.2.cloned.1.call-done = bf16[512,2048]{1,0:T(8,128)(2,1)} async-done(((bf16[64,2048]{1,0:T(8,128)(2,1)}), bf16[512,2048]{1,0:T(8,128)(2,1)}) %all-gather.2.cloned.1.call-update) | async-done | bytes 2097168 | tf_op jit(solution)/shard_map/all_gather | solution.py:99
  338.1 5.2 %fusion.43 = f32[512,704]{0,1:T(8,128)} fusion(bf16[512,2048]{1,0:T(8,128)(2,1)} %all-gather.2.cloned.1.call-done, bf16[2048,704]{0,1:T(8,128)(2,1)} %param.25), kind=kOutput, calls=%fused_computation.61 | convolution fusion | flops 1476395008 | bytes 6422528 | tf_op jit(solution)/shard_map/dot_general | solution.py:100
  343.3 0.0 copy-done
  343.3 7.7 %convolution_convert_fusion.1 = bf16[512,2048]{1,0:T(8,128)(2,1)} fusion(bf16[704,2048]{1,0:T(8,128)(2,1)S(1)} %copy-done, bf16[512,2048]{1,0:T(8,128)(2,1)} %all-gather.2.cloned.1.call-done, bf16[2048,704]{0,1:T(8,128)(2,1)} %param.26, f32[512,704]{0,1:T(8,128)} %fusion.43), kind=kOutput, calls=%fused_computation.17 | convolution fusion | flops 2956001280 | bytes 11403264 | tf_op jit(solution)/shard_map/dot_general | solution.py:105
  351.1 0.0 reduce-scatter.5.cloned.1.call-update
  351.1 0.0 copy-done.2
  351.1 1.2 fusion.44
  352.3 0.1 select_reduce_fusion.1
  352.4 0.1 select_reduce_fusion
  352.6 0.2 fusion.23
  352.7 153.1 %all-to-all-done.1 = bf16[32,8,8,2048]{3,2,1,0:T(8,128)(2,1)} async-done(((bf16[32,8,8,2048]{3,2,1,0:T(8,128)(2,1)}), bf16[32,8,8,2048]{3,2,1,0:T(8,128)(2,1)}, u32[]{:S(2)}, u32[]{:S(2)}) %all-to-all-start.1) | async-done | bytes 8388640 | tf_op jit(solution)/shard_map/all_to_all | solution.py:89
  505.8 7.3 %reduce_sum.81 = bf16[8,8,8,2048]{3,2,1,0:T(8,128)(2,1)} reduce(bf16[4,8,8,8,2048]{4,3,2,1,0:T(8,128)(2,1)} %bitcast.15, bf16[]{:T(256)} %constant.24.clone.1), dimensions={0}, to_apply=%region_11.12 | reduce | flops 3145728 | bytes 10485762 | tf_op jit(solution)/shard_map/reduce_sum | solution.py:92
  513.1 2.2 fusion.24
  515.3 0.0 copy-start.5
  515.4 0.8 fusion.32
  (19 shorter events, 0.1 us)
Async XLA Ops:
  7.2 336.2 %copy-start = (bf16[704,2048]{1,0:T(8,128)(2,1)S(1)}, bf16[704,2048]{1,0:T(8,128)(2,1)}, u32[]{:S(2)}) copy-start(bf16[704,2048]{1,0:T(8,128)(2,1)} %param.27) | copy-start | bytes 8650756
  7.2 3.6 copy-start.6
  7.2 4.1 copy-start.7
  7.2 4.1 copy-start.10
  7.2 34.2 %copy-start.3 = (bf16[1,64,2048]{2,1,0:T(8,128)(2,1)S(1)}, bf16[1,64,2048]{2,1,0:T(8,128)(2,1)}, u32[]{:S(2)}) copy-start(bf16[1,64,2048]{2,1,0:T(8,128)(2,1)} %param.16) | copy-start | bytes 786436
  7.2 34.2 %reduce-scatter.3.cloned.1.call-start = ((), (), s32[]{:S(2)}) async-start(), calls=%async_computation.4 | async-start | bytes 1310720 | tf_op jit(solution)/shard_map/reduce_scatter | solution.py:46
  43.6 1.9 copy-start.1
  280.7 225.1 %all-to-all-start.1 = ((bf16[32,8,8,2048]{3,2,1,0:T(8,128)(2,1)}), bf16[32,8,8,2048]{3,2,1,0:T(8,128)(2,1)}, u32[]{:S(2)}, u32[]{:S(2)}) async-start(bf16[32,8,8,2048]{3,2,1,0:T(8,128)(2,1)} %copy.34), calls=%async_computation.3 | async-start | bytes 16777216 | tf_op jit(solution)/shard_map/all_to_all | solution.py:89
  284.4 53.7 %all-gather.2.cloned.1.call-start = ((), (), s32[]{:S(2)}) async-start(), calls=%async_computation.5 | async-start | bytes 2359296 | tf_op jit(solution)/shard_map/all_gather | solution.py:99
  285.2 227.9 %reduce-scatter.5.cloned.1.call-start = ((), (), s32[]{:S(2)}) async-start(), calls=%async_computation.6 | async-start | bytes 2359296 | tf_op jit(solution)/shard_map/reduce_scatter | solution.py:104
  343.3 7.7 %copy-start.8 = (bf16[2048]{0:T(1024)(128)(2,1)S(1)}, bf16[2048]{0:T(1024)(128)(2,1)}, u32[]{:S(2)}) copy-start(bf16[2048]{0:T(1024)(128)(2,1)} %param.28) | copy-start | bytes 12292
  343.3 7.8 %copy-start.9 = (bf16[2048]{0:T(1024)(128)(2,1)S(1)}, bf16[2048]{0:T(1024)(128)(2,1)}, u32[]{:S(2)}) copy-start(bf16[2048]{0:T(1024)(128)(2,1)} %param.29) | copy-start | bytes 12292
  343.3 7.8 %copy-start.2 = (bf16[64,2048]{1,0:T(8,128)(2,1)S(1)}, bf16[64,2048]{1,0:T(8,128)(2,1)}, u32[]{:S(2)}) copy-start(bf16[64,2048]{1,0:T(8,128)(2,1)} %copy-done.1) | copy-start | bytes 786436
  505.8 7.3 %copy-start.4 = (bf16[64,2048]{1,0:T(8,128)(2,1)S(1)}, bf16[64,2048]{1,0:T(8,128)(2,1)}, u32[]{:S(2)}) copy-start(bf16[64,2048]{1,0:T(8,128)(2,1)} %reduce-scatter.3.cloned.1.call-done) | copy-start | bytes 786436
  515.3 0.9 copy-start.5
Sparse Core Ops, SparseCore 0:
  10.9 30.4 reduce-scatter.2
  287.5 50.5 all-gather.1
  351.2 73.7 reduce-scatter.4
where the time goes:
time: 523 us
  waiting for transfers between devices  236 us (45%)
  blocking collectives  189 us (36%)
  matrix products  58.4 us (11%)
  between operations  14 us (3%)
  other arithmetic  11.1 us (2%)
  local copies, waits for them, and re-layouts  9.59 us (2%)
    all_to_all x1, blocking collectives, per_device(): lax.all_to_all(copies, ('dp', 'ep'), split_axis=0, concat_axis=0, tiled=T...  189 us
    all_to_all x1, waiting for transfers between devices, per_device(): lax.all_to_all(partial_value, ('dp', 'ep'), split_axis=0, concat_axis=0,...  153 us
    all_gather x1, waiting for transfers between devices, per_device(): row_block = lax.all_gather(normed, 'ep', axis=0, tiled=True)  52.7 us
    reduce_scatter x1, waiting for transfers between devices, per_device(): lax.psum_scatter(jnp.dot(row_block, w_out, preferred_element_type=jnp.flo...  29.8 us
    dot_general x1, matrix products, expert_partial(): jnp.einsum('semf,efd->semd', hidden, w_down, preferred_element_type=jnp.f...  23.5 us
    dot_general x1, matrix products, expert_partial(): jnp.einsum('semd,edf->semf', rows_in, w_gate, preferred_element_type=jnp....  14.1 us
  transfers between devices with their start and end apart: 4, of which 3 were waited for; matrix products, arithmetic and copies ran while one was open for 4% of the time, Pallas kernels for 0%

commit v1 on v0

--- a/solution.py
+++ b/solution.py
@@ -96,7 +96,12 @@
     routed = jnp.dot(
         combine_mat, returned.reshape(buffer_cells, model_width), preferred_element_type=jnp.float32
     )
-    row_block = lax.all_gather(normed, "ep", axis=0, tiled=True)
+    ring = [normed]
+    for hop in range(7):
+        ring.append(lax.ppermute(ring[-1], "ep", [(dev, (dev + 1) % 8) for dev in range(8)]))
+    row_block = jnp.roll(
+        jnp.concatenate(ring[::-1], axis=0), (lax.axis_index("ep") + 1) * ring[0].shape[0], axis=0
+    )
     gate_part = jnp.dot(row_block, w_shared_gate, preferred_element_type=jnp.float32)
     up_part = jnp.dot(row_block, w_shared_up, preferred_element_type=jnp.float32)
     hidden_all = (jax.nn.silu(gate_part) * up_part).astype(jnp.bfloat16)

time: 523 us -> 575 us (1.099)
  starting transfers between devices: 3.97 us -> 42.2 us
  local copies, waits for them, and re-layouts: 9.59 us -> 23.9 us
    ppermute x0 -> x7, waiting for transfers between devices: none -> 175 us  [per_device(): lax.ppermute(ring[-1], 'ep', [(dev, (dev + 1) % 8) for dev in range(8)])]
    all_to_all x1, waiting for transfers between devices: 153 us -> 0.01 us  [per_device(): lax.all_to_all(partial_value, ('dp', 'ep'), split_axis=0, concat_axis=0,...]
    all_gather x1 -> x0, waiting for transfers between devices: 52.7 us -> none  [per_device(): row_block = lax.all_gather(normed, 'ep', axis=0, tiled=True)]
    ppermute x0 -> x7, starting transfers between devices: none -> 38.4 us  [per_device(): lax.ppermute(ring[-1], 'ep', [(dev, (dev + 1) % 8) for dev in range(8)])]
    reduce_scatter x1, waiting for transfers between devices: 0.01 us -> 32.5 us  [per_device(): lax.psum_scatter(jnp.dot(row_block, w_shared_down, preferred_element_type...]
    unnamed x23 -> x58, local copies, waits for them, and re-layouts: 0.06 us -> 14.3 us
  transfers between devices with their start and end apart: 4 -> 10, of which waited for: 3 -> 9; matrix products, arithmetic and copies ran while one was open for 4% -> 5% of each run, Pallas kernels for 0% -> 0%
where the time goes in v1:
time: 575 us
  waiting for transfers between devices  238 us (41%)
  blocking collectives  189 us (33%)
  matrix products  56 us (10%)
  starting transfers between devices  42.2 us (7%)
  local copies, waits for them, and re-layouts  23.9 us (4%)
  between operations  14.4 us (3%)
  other arithmetic  11.1 us (2%)
    all_to_all x1, blocking collectives, per_device(): lax.all_to_all(copies, ('dp', 'ep'), split_axis=0, concat_axis=0, tiled=T...  189 us
    ppermute x7, waiting for transfers between devices, per_device(): lax.ppermute(ring[-1], 'ep', [(dev, (dev + 1) % 8) for dev in range(8)])  175 us
    ppermute x7, starting transfers between devices, per_device(): lax.ppermute(ring[-1], 'ep', [(dev, (dev + 1) % 8) for dev in range(8)])  38.4 us
    reduce_scatter x1, waiting for transfers between devices, per_device(): lax.psum_scatter(jnp.dot(row_block, w_shared_down, preferred_element_type...  32.5 us
    reduce_scatter x1, waiting for transfers between devices, per_device(): lax.psum_scatter(jnp.dot(row_block, w_out, preferred_element_type=jnp.flo...  29.8 us
    dot_general x1, matrix products, expert_partial(): jnp.einsum('semf,efd->semd', hidden, w_down, preferred_element_type=jnp.f...  23.5 us
    unnamed x58, local copies, waits for them, and re-layouts  14.3 us
    dot_general x1, matrix products, expert_partial(): jnp.einsum('semd,edf->semf', rows_in, w_gate, preferred_element_type=jnp....  14.1 us
  transfers between devices with their start and end apart: 10, of which 9 were waited for; matrix products, arithmetic and copies ran while one was open for 5% of the time, Pallas kernels for 0%

profile of v1, /device:TPU:0, one launch (start us, length us, event | category | flops | bytes accessed | tf_op | source)
XLA Modules:
  0.0 574.8 jit_solution(17200336297412271853)
XLA Ops:
  7.3 3.5 convolution_convert_fusion.2
  11.3 0.1 select_reduce_fusion.3
  11.4 0.1 fusion.39
  11.6 29.8 %reduce-scatter.3.cloned.1.call-done = bf16[64,2048]{1,0:T(8,128)(2,1)} async-done(((bf16[256,2048]{1,0:T(8,128)(2,1)}), bf16[64,2048]{1,0:T(8,128)(2,1)}) %reduce-scatter.3.cloned.1.call-update) | async-done | bytes 262160 | tf_op jit(solution)/shard_map/reduce_scatter | solution.py:46
  41.4 1.1 fusion.35
  42.5 1.1 fusion.37
  43.6 0.8 convolution_convert_fusion
  44.4 1.1 broadcast_in_dim.80
  45.5 189.4 %all_to_all.10 = bf16[32,8,8,2048]{3,2,1,0:T(8,128)(2,1)} all-to-all(bf16[32,8,8,2048]{3,2,1,0:T(8,128)(2,1)S(1)} %bitcast.86), channel_id=1, replica_groups=mesh['dp'=4,'ep'=8] {'dp','ep'}, dimensions={0} | all-to-all | bytes 16777216 | tf_op jit(solution)/shard_map/all_to_all | solution.py:84
  234.9 14.1 %fusion.4 = f32[8,32,8,352]{3,2,1,0:T(8,128)} fusion(bf16[8,2048,352]{1,2,0:T(8,128)(2,1)} %param.22, bf16[32,8,8,2048]{3,2,1,0:T(8,128)(2,1)} %all_to_all.10), kind=kOutput, calls=%fused_computation.4 | convolution fusion | flops 2952790016 | bytes 22806528 | tf_op jit(solution)/shard_map/semd,edf->semf/dot_general | solution.py:20
  249.0 23.5 %convert_bitcast_fusion = bf16[32,8,8,2048]{3,2,0,1:T(8,128)(2,1)} fusion(bf16[8,352,2048]{2,1,0:T(8,128)(2,1)} %param.24, f32[8,32,8,352]{3,2,1,0:T(8,128)} %fusion.4, bf16[8,2048,352]{1,2,0:T(8,128)(2,1)} %param.23, bf16[32,8,8,2048]{3,2,1,0:T(8,128)(2,1)} %all_to_all.10), kind=kOutput, calls=%fused_computation.6 | convolution fusion | flops 5914099712 | bytes 42729472 | tf_op jit(solution)/shard_map/semf,efd->semd/dot_general | solution.py:23
  272.5 8.3 %copy.34 = bf16[32,8,8,2048]{3,2,1,0:T(8,128)(2,1)} copy(bf16[32,8,8,2048]{3,2,0,1:T(8,128)(2,1)} %convert_bitcast_fusion) | data formatting | bytes 16777216 | tf_op jit(solution)/shard_map/convert_element_type | solution.py:88
  280.7 3.7 all-to-all-start.1
  284.5 143.2 %collective-permute-done = bf16[64,2048]{1,0:T(8,128)(2,1)S(1)} collective-permute-done((bf16[64,2048]{1,0:T(8,128)(2,1)S(1)}, bf16[64,2048]{1,0:T(8,128)(2,1)S(1)}, u32[]{:S(2)}, u32[]{:S(2)}) %collective-permute-start) | collective-permute-done | bytes 262176 | tf_op jit(solution)/shard_map/ppermute | solution.py:101
  427.7 0.7 copy-done.4
  428.4 7.7 %collective-permute-done.1 = bf16[64,2048]{1,0:T(8,128)(2,1)S(1)} collective-permute-done((bf16[64,2048]{1,0:T(8,128)(2,1)S(1)}, bf16[64,2048]{1,0:T(8,128)(2,1)S(1)}, u32[]{:S(2)}, u32[]{:S(2)}) %collective-permute-start.1) | collective-permute-done | bytes 262176 | tf_op jit(solution)/shard_map/ppermute | solution.py:101
  436.1 0.7 copy-done.6
  436.8 7.7 %collective-permute-done.2 = bf16[64,2048]{1,0:T(8,128)(2,1)S(1)} collective-permute-done((bf16[64,2048]{1,0:T(8,128)(2,1)S(1)}, bf16[64,2048]{1,0:T(8,128)(2,1)S(1)}, u32[]{:S(2)}, u32[]{:S(2)}) %collective-permute-start.2) | collective-permute-done | bytes 262176 | tf_op jit(solution)/shard_map/ppermute | solution.py:101
  444.5 0.7 copy-done.8
  445.2 30.5 %collective-permute-start.3 = (bf16[64,2048]{1,0:T(8,128)(2,1)S(1)}, bf16[64,2048]{1,0:T(8,128)(2,1)S(1)}, u32[]{:S(2)}, u32[]{:S(2)}) collective-permute-start(bf16[64,2048]{1,0:T(8,128)(2,1)S(1)} %collective-permute-done.2), channel_id=1, source_target_pairs={{0,1},{1,2},{2,3},{3,4},{4,5},{5,6},{6,7},{7,0},{8,9},{9,10},{10,1... | collective-permute-start | bytes 786440 | tf_op jit(solution)/shard_map/ppermute | solution.py:101
  475.8 1.2 collective-permute-done.3
  476.9 0.7 copy-done.10
  477.6 4.6 collective-permute-start.4
  482.3 3.3 collective-permute-done.4
  485.5 0.7 copy-done.12
  486.2 2.5 collective-permute-start.5
  488.8 5.2 collective-permute-done.5
  493.9 0.6 collective-permute-start.6
  494.6 7.2 %collective-permute-done.6 = bf16[64,2048]{1,0:T(8,128)(2,1)} collective-permute-done((bf16[64,2048]{1,0:T(8,128)(2,1)}, bf16[64,2048]{1,0:T(8,128)(2,1)}, u32[]{:S(2)}, u32[]{:S(2)}) %collective-permute-start.6) | collective-permute-done | bytes 262176 | tf_op jit(solution)/shard_map/ppermute | solution.py:101
  501.9 1.0 constant_dynamic-update-slice_fusion.15
  502.8 1.0 constant_dynamic-update-slice_fusion.14
  503.8 1.0 constant_dynamic-update-slice_fusion.13
  504.8 1.0 constant_dynamic-update-slice_fusion.12
  505.7 1.0 constant_dynamic-update-slice_fusion.11
  506.7 1.0 constant_dynamic-update-slice_fusion.10
  507.7 1.0 constant_dynamic-update-slice_fusion.9
  508.7 1.0 constant_dynamic-update-slice_fusion.7
  509.7 1.0 constant_dynamic-update-slice_fusion.6
  510.9 1.9 copy-done.15
  512.8 2.8 fusion.19
  515.6 7.7 %convolution_convert_fusion.1 = bf16[512,2048]{1,0:T(8,128)(2,1)} fusion(bf16[704,2048]{1,0:T(8,128)(2,1)S(1)} %copy-done, f32[512,704]{0,1:T(8,128)} %fusion.19, bf16[2048,704]{0,1:T(8,128)(2,1)} %param.25, bf16[1024,2048]{1,0:T(8,128)(2,1)} %copy-done.15, s32[]{:T(128)S(6)} %select_n.30), kind=kOutput, calls=%fused_computation.17 | convolution fusion | flops 2956001280 | bytes 11403268 | tf_op jit(solution)/shard_map/dot_general | solution.py:110
  523.4 1.2 fusion.54
  524.7 0.1 select_reduce_fusion
  524.8 0.2 fusion.26
  525.0 7.3 %reduce_sum.81 = bf16[8,8,8,2048]{3,2,1,0:T(8,128)(2,1)} reduce(bf16[4,8,8,8,2048]{4,3,2,1,0:T(8,128)(2,1)} %bitcast.15, bf16[]{:T(256)} %constant.53.clone.1), dimensions={0}, to_apply=%region_11.12 | reduce | flops 3145728 | bytes 10485762 | tf_op jit(solution)/shard_map/reduce_sum | solution.py:92
  532.3 32.5 %reduce-scatter.5.cloned.1.call-done = bf16[64,2048]{1,0:T(8,128)(2,1)} async-done(((bf16[512,2048]{1,0:T(8,128)(2,1)}), bf16[64,2048]{1,0:T(8,128)(2,1)}) %reduce-scatter.5.cloned.1.call-update) | async-done | bytes 262160 | tf_op jit(solution)/shard_map/reduce_scatter | solution.py:109
  564.8 2.2 fusion.32
  567.1 0.8 fusion.40
  (66 shorter events, 1.0 us)
Async XLA Ops:
  7.2 508.4 %copy-start = (bf16[704,2048]{1,0:T(8,128)(2,1)S(1)}, bf16[704,2048]{1,0:T(8,128)(2,1)}, u32[]{:S(2)}) copy-start(bf16[704,2048]{1,0:T(8,128)(2,1)} %param.27) | copy-start | bytes 8650756
  7.2 3.6 copy-start.16
  7.2 3.6 copy-start.14
  7.2 4.1 copy-start.19
  7.2 34.2 %copy-start.1 = (bf16[1,64,2048]{2,1,0:T(8,128)(2,1)S(1)}, bf16[1,64,2048]{2,1,0:T(8,128)(2,1)}, u32[]{:S(2)}) copy-start(bf16[1,64,2048]{2,1,0:T(8,128)(2,1)} %param.16) | copy-start | bytes 786436
  7.2 34.2 %reduce-scatter.3.cloned.1.call-start = ((), (), s32[]{:S(2)}) async-start(), calls=%async_computation.4 | async-start | bytes 1310720 | tf_op jit(solution)/shard_map/reduce_scatter | solution.py:46
  280.7 244.3 %all-to-all-start.1 = ((bf16[32,8,8,2048]{3,2,1,0:T(8,128)(2,1)}), bf16[32,8,8,2048]{3,2,1,0:T(8,128)(2,1)}, u32[]{:S(2)}, u32[]{:S(2)}) async-start(bf16[32,8,8,2048]{3,2,1,0:T(8,128)(2,1)} %copy.34), calls=%async_computation.3 | async-start | bytes 16777216 | tf_op jit(solution)/shard_map/all_to_all | solution.py:89
  284.4 280.4 %reduce-scatter.5.cloned.1.call-start = ((), (), s32[]{:S(2)}) async-start(), calls=%async_computation.5 | async-start | bytes 2359296 | tf_op jit(solution)/shard_map/reduce_scatter | solution.py:109
  284.5 143.3 %collective-permute-start = (bf16[64,2048]{1,0:T(8,128)(2,1)S(1)}, bf16[64,2048]{1,0:T(8,128)(2,1)S(1)}, u32[]{:S(2)}, u32[]{:S(2)}) collective-permute-start(bf16[64,2048]{1,0:T(8,128)(2,1)S(1)} %fusion.37), channel_id=1, source_target_pairs={{0,1},{1,2},{2,3},{3,4},{4,5},{5,6},{6,7},{7,0},{8,9},{9,10},{10,1... | collective-permute-start | bytes 786440 | tf_op jit(solution)/shard_map/ppermute | solution.py:101
  427.7 0.7 copy-start.4
  428.4 7.7 %collective-permute-start.1 = (bf16[64,2048]{1,0:T(8,128)(2,1)S(1)}, bf16[64,2048]{1,0:T(8,128)(2,1)S(1)}, u32[]{:S(2)}, u32[]{:S(2)}) collective-permute-start(bf16[64,2048]{1,0:T(8,128)(2,1)S(1)} %collective-permute-done), channel_id=1, source_target_pairs={{0,1},{1,2},{2,3},{3,4},{4,5},{5,6},{6,7},{7,0},{8,9},{9,10},{10,1... | collective-permute-start | bytes 786440 | tf_op jit(solution)/shard_map/ppermute | solution.py:101
  436.1 0.7 copy-start.6
  436.8 7.7 %collective-permute-start.2 = (bf16[64,2048]{1,0:T(8,128)(2,1)S(1)}, bf16[64,2048]{1,0:T(8,128)(2,1)S(1)}, u32[]{:S(2)}, u32[]{:S(2)}) collective-permute-start(bf16[64,2048]{1,0:T(8,128)(2,1)S(1)} %collective-permute-done.1), channel_id=1, source_target_pairs={{0,1},{1,2},{2,3},{3,4},{4,5},{5,6},{6,7},{7,0},{8,9},{9,10},{10,1... | collective-permute-start | bytes 786440 | tf_op jit(solution)/shard_map/ppermute | solution.py:101
  444.5 0.7 copy-start.8
  445.2 31.7 %collective-permute-start.3 = (bf16[64,2048]{1,0:T(8,128)(2,1)S(1)}, bf16[64,2048]{1,0:T(8,128)(2,1)S(1)}, u32[]{:S(2)}, u32[]{:S(2)}) collective-permute-start(bf16[64,2048]{1,0:T(8,128)(2,1)S(1)} %collective-permute-done.2), channel_id=1, source_target_pairs={{0,1},{1,2},{2,3},{3,4},{4,5},{5,6},{6,7},{7,0},{8,9},{9,10},{10,1... | collective-permute-start | bytes 786440 | tf_op jit(solution)/shard_map/ppermute | solution.py:101
  476.9 0.7 copy-start.10
  477.6 7.9 %collective-permute-start.4 = (bf16[64,2048]{1,0:T(8,128)(2,1)S(1)}, bf16[64,2048]{1,0:T(8,128)(2,1)S(1)}, u32[]{:S(2)}, u32[]{:S(2)}) collective-permute-start(bf16[64,2048]{1,0:T(8,128)(2,1)S(1)} %collective-permute-done.3), channel_id=1, source_target_pairs={{0,1},{1,2},{2,3},{3,4},{4,5},{5,6},{6,7},{7,0},{8,9},{9,10},{10,1... | collective-permute-start | bytes 786440 | tf_op jit(solution)/shard_map/ppermute | solution.py:101
  485.5 0.7 copy-start.12
  486.2 7.7 %collective-permute-start.5 = (bf16[64,2048]{1,0:T(8,128)(2,1)S(1)}, bf16[64,2048]{1,0:T(8,128)(2,1)}, u32[]{:S(2)}, u32[]{:S(2)}) collective-permute-start(bf16[64,2048]{1,0:T(8,128)(2,1)S(1)} %collective-permute-done.4), channel_id=1, source_target_pairs={{0,1},{1,2},{2,3},{3,4},{4,5},{5,6},{6,7},{7,0},{8,9},{9,10},{10,1... | collective-permute-start | bytes 786440 | tf_op jit(solution)/shard_map/ppermute | solution.py:101
  493.9 7.9 %collective-permute-start.6 = (bf16[64,2048]{1,0:T(8,128)(2,1)}, bf16[64,2048]{1,0:T(8,128)(2,1)}, u32[]{:S(2)}, u32[]{:S(2)}) collective-permute-start(bf16[64,2048]{1,0:T(8,128)(2,1)} %collective-permute-done.5), channel_id=1, source_target_pairs={{0,1},{1,2},{2,3},{3,4},{4,5},{5,6},{6,7},{7,0},{8,9},{9,10},{10,1... | collective-permute-start | bytes 786440 | tf_op jit(solution)/shard_map/ppermute | solution.py:101
  494.6 16.1 %copy-start.13 = (bf16[64,2048]{1,0:T(8,128)(2,1)S(1)}, bf16[64,2048]{1,0:T(8,128)(2,1)}, u32[]{:S(2)}) copy-start(bf16[64,2048]{1,0:T(8,128)(2,1)} %copy-done.12) | copy-start | bytes 786436
  494.6 16.1 %copy-start.11 = (bf16[64,2048]{1,0:T(8,128)(2,1)S(1)}, bf16[64,2048]{1,0:T(8,128)(2,1)}, u32[]{:S(2)}) copy-start(bf16[64,2048]{1,0:T(8,128)(2,1)} %copy-done.10) | copy-start | bytes 786436
  494.6 16.1 %copy-start.9 = (bf16[64,2048]{1,0:T(8,128)(2,1)S(1)}, bf16[64,2048]{1,0:T(8,128)(2,1)}, u32[]{:S(2)}) copy-start(bf16[64,2048]{1,0:T(8,128)(2,1)} %copy-done.8) | copy-start | bytes 786436
  494.6 16.2 %copy-start.7 = (bf16[64,2048]{1,0:T(8,128)(2,1)S(1)}, bf16[64,2048]{1,0:T(8,128)(2,1)}, u32[]{:S(2)}) copy-start(bf16[64,2048]{1,0:T(8,128)(2,1)} %copy-done.6) | copy-start | bytes 786436
  494.6 16.2 %copy-start.5 = (bf16[64,2048]{1,0:T(8,128)(2,1)S(1)}, bf16[64,2048]{1,0:T(8,128)(2,1)}, u32[]{:S(2)}) copy-start(bf16[64,2048]{1,0:T(8,128)(2,1)} %copy-done.4) | copy-start | bytes 786436
  494.6 18.2 %copy-start.20 = (bf16[2048,704]{0,1:T(8,128)(2,1)S(1)}, bf16[2048,704]{0,1:T(8,128)(2,1)}, u32[]{:S(2)}) copy-start(bf16[2048,704]{0,1:T(8,128)(2,1)} %param.26) | copy-start | bytes 8650756
  510.9 1.9 copy-start.15
  515.6 7.8 %copy-start.17 = (bf16[2048]{0:T(1024)(128)(2,1)S(1)}, bf16[2048]{0:T(1024)(128)(2,1)}, u32[]{:S(2)}) copy-start(bf16[2048]{0:T(1024)(128)(2,1)} %param.28) | copy-start | bytes 12292
  515.6 7.8 %copy-start.18 = (bf16[2048]{0:T(1024)(128)(2,1)S(1)}, bf16[2048]{0:T(1024)(128)(2,1)}, u32[]{:S(2)}) copy-start(bf16[2048]{0:T(1024)(128)(2,1)} %param.29) | copy-start | bytes 12292
  525.0 39.8 %copy-start.2 = (bf16[64,2048]{1,0:T(8,128)(2,1)S(1)}, bf16[64,2048]{1,0:T(8,128)(2,1)}, u32[]{:S(2)}) copy-start(bf16[64,2048]{1,0:T(8,128)(2,1)} %reduce-scatter.3.cloned.1.call-done) | copy-start | bytes 786436
  567.1 0.9 copy-start.3
Sparse Core Ops, SparseCore 0:
  10.9 30.4 reduce-scatter.2
  523.5 41.3 reduce-scatter.4
